TPU v7x, 1024 devices: a whole 4x4x32 slice. The times are simulated.
1024 devices in a mesh: dp: 4 (over x), ctx: 32 (over z), tp: 8 (over y, core).
Axes of the slice: x: 4, y: 4, z: 32, core: 2. Of those that a mesh axis runs over, the one named last changes fastest.
Arguments:
- queries: bfloat16 [16384, 4096], P(('dp', 'ctx'), 'tp'), parts along dimension 0, may hold values from -25 to 25
- keys: bfloat16 [16384, 1024], P(('dp', 'ctx'), 'tp'), parts along dimension 0, may hold values from -6 to 6
- values: bfloat16 [16384, 1024], P(('dp', 'ctx'), 'tp'), parts along dimension 0, may hold values from -6 to 6
- counts: int32 [128, 32], P('dp'), parts along dimension 0, may hold values from 0 to 8, as said below
- doc_lengths: int32 [64], P('dp'), parts along dimension 0, may hold values from 1 to 2048, 4096 in all
Outputs:
- attended: bfloat16 [16384, 4096], P(('dp', 'ctx'), 'tp'), parts along dimension 0
There are 4 independent parts, one for each index of `dp`. A program takes and returns all parts, laid end to end along the dimension named above; each array names one. Nothing has to cross between parts.
Inputs may be any that keep to these rules, and one draw needn't show every extreme that they name: Every row and every column of counts sums to 128; no entry exceeds 8, and some entry equals 8.
All inputs are finite; a program needn't handle non-finite values.
Results may differ from a plain program's by a relative error of at most 0.006.
Values may be sent and summed in bfloat16 or wider, within the bound.
No kernel may reach another device: no remote copies, remote signals or barrier semaphores. Data moves between devices by JAX's collectives and lax.ppermute only.
A program may use at most 32 MiB of HBM per device.

v0:
```python
import functools

import jax
import jax.numpy as jnp
from jax import lax
from jax.experimental import pallas as pl
from jax.experimental.pallas import tpu as pltpu
from jax.sharding import PartitionSpec as P

HQ = 32
KVH = 8
HD = 128
GROUP = HQ // KVH
TOK = 128
HALF = 64
NCX = 32
SLOT = 8
KEYS = NCX // 2 * TOK
MAIN = 124
REST = TOK - MAIN
C2 = 1.4426950408889634 / HD**0.5
NEG = -1e30
SIDES = [list(range(0, NCX, 2)), list(range(1, NCX, 2))]

f32 = jnp.float32
bf16 = jnp.bfloat16
i32 = jnp.int32


def iota(shape, dim):
    return lax.broadcasted_iota(i32, shape, dim)


def pack_kernel(counts_ref, q_ref, k_ref, v_ref, out_ref, kv_ref):
    me = lax.axis_index("ctx")
    row = counts_ref[pl.ds(me, 1), :].astype(f32)
    slots = NCX * SLOT
    owner_of = iota((slots, NCX), 0) // SLOT
    owner = iota((slots, NCX), 1)
    start = jnp.sum(jnp.where(owner < owner_of, row, 0.0), axis=1, keepdims=True)
    count = jnp.sum(jnp.where(owner == owner_of, row, 0.0), axis=1, keepdims=True)
    j = iota((slots, 1), 0) % SLOT
    jf = j.astype(f32)
    want = jnp.where(jf < count, start + jf, -1.0)
    lane = iota((slots, TOK), 1)
    pick = jnp.where(lane.astype(f32) == want, 1.0, 0.0).astype(bf16)
    wide = GROUP * HD
    out_ref[:, :wide] = jnp.dot(pick, q_ref[...], preferred_element_type=f32).astype(bf16)
    pick_k = jnp.where(lane == jnp.where(j < REST, MAIN + j, -1), 1.0, 0.0).astype(bf16)
    pick_v = jnp.where(lane == jnp.where(j >= REST, MAIN + j - REST, -1), 1.0, 0.0).astype(bf16)
    rest = jnp.dot(pick_k, k_ref[...], preferred_element_type=f32)
    rest = rest + jnp.dot(pick_v, v_ref[...], preferred_element_type=f32)
    out_ref[:, wide:] = rest.astype(bf16)
    kv_ref[:, :HD] = k_ref[:MAIN, :]
    kv_ref[:, HD:] = v_ref[:MAIN, :]


def place_kernel(counts_ref, pos_ref):
    counts = counts_ref[...].astype(f32)
    a, b = iota((NCX, NCX), 0), iota((NCX, NCX), 1)
    starts = jnp.dot(counts, (a < b).astype(f32), preferred_element_type=f32)
    before = jnp.dot((b < a).astype(f32), counts, preferred_element_type=f32)
    row = iota((NCX, TOK), 1).astype(f32)
    pos = jnp.zeros((NCX, TOK), f32)
    for o in range(NCX):
        j = row - starts[:, o : o + 1]
        local = before[:, o : o + 1] + j
        here = jnp.where(local < HALF, local + o * HALF, local + ((2 * NCX - 1 - o) * HALF - HALF))
        pos = jnp.where((j >= 0) & (j < counts[:, o : o + 1]), here, pos)
    pos_ref[:NCX, :] = pos
    parity = lax.axis_index("ctx") % 2
    loader, lane = iota((NCX, TOK), 0), iota((NCX, TOK), 1)
    rest = jnp.zeros((NCX, TOK), f32)
    for r in range(REST):
        here = (loader == 2 * (lane // REST) + parity) & (lane % REST == r)
        rest = jnp.where(here, pos[:, MAIN + r : MAIN + r + 1], rest)
    pos_ref[NCX:, :] = jnp.broadcast_to(jnp.sum(rest, axis=0, keepdims=True), (8, TOK))


def unpack_kernel(counts_ref, got_ref, out_ref, rest_ref):
    me = lax.axis_index("ctx")
    slots = NCX * SLOT
    counts = counts_ref[...].astype(f32)
    mine = jnp.sum(jnp.where(iota((NCX, NCX), 1) == me, counts, 0.0), axis=1, keepdims=True)
    src_of, src = iota((NCX, slots), 1) // SLOT, iota((NCX, slots), 0)
    before = jnp.sum(jnp.where(src < src_of, mine, 0.0), axis=0, keepdims=True)
    count = jnp.sum(jnp.where(src == src_of, mine, 0.0), axis=0, keepdims=True)
    j = (iota((1, slots), 1) % SLOT).astype(f32)
    local = jnp.where(j < count, before + j, -1.0)
    pick = jnp.where(iota((TOK, slots), 0).astype(f32) == local, 1.0, 0.0).astype(bf16)
    wide = GROUP * HD
    out_ref[...] = jnp.dot(pick, got_ref[:, :wide], preferred_element_type=f32).astype(bf16)
    n = NCX // 2 * REST
    row, slot = iota((n, slots), 0), iota((n, slots), 1)
    at = (2 * (row // REST) + me % 2) * SLOT + row % REST
    for c in range(2):
        pick = jnp.where(slot == at + c * REST, 1.0, 0.0).astype(bf16)
        rest = jnp.dot(pick, got_ref[:, wide:], preferred_element_type=f32)
        rest_ref[:, c * HD : (c + 1) * HD] = rest.astype(bf16)


def attend_kernel(flip, docs_ref, pos_ref, q_ref, kv_ref, rest_ref, out_ref, s_ref, top_ref, acc_ref, sum_ref):
    me = lax.axis_index("ctx")
    parity = me % 2
    owner = me + flip * (1 - 2 * parity)
    q_id = iota((TOK, HD), 0)
    q_pos = jnp.where(q_id < HALF, owner * HALF + q_id, (2 * NCX - 1 - owner) * HALF + q_id - HALF)
    q_first = jnp.zeros((TOK, HD), i32)
    end = jnp.int32(0)
    for d in range(docs_ref.shape[0]):
        end = end + docs_ref[d]
        q_first = jnp.where(q_pos >= end, end, q_first)
    q_pos, q_first = q_pos.astype(f32), q_first.astype(f32)

    blocks = [(i, MAIN) for i in range(NCX // 2)] + [(NCX // 2, NCX // 2 * REST)]

    def rows(i, cols):
        return kv_ref[i, :, cols] if i < NCX // 2 else rest_ref[:, cols]

    top_ref[...] = jnp.full(top_ref.shape, NEG, f32)
    for i, n in blocks:
        keys = rows(i, slice(0, HD))
        k_pos = pos_ref[pl.ds(2 * i + parity, 1), :] if i < NCX // 2 else pos_ref[NCX : NCX + 1, :]
        seen = ((k_pos <= q_pos) & (k_pos >= q_first))[:, :n]
        for h in range(GROUP):
            s = lax.dot_general(
                q_ref[:, h * HD : (h + 1) * HD], keys, (((1,), (1,)), ((), ())), preferred_element_type=f32
            )
            part = jnp.where(seen, s, NEG)
            s_ref[h, :, i * TOK : i * TOK + n] = part
            top_ref[h, :, :n] = jnp.maximum(top_ref[h, :, :n], part)
    for h in range(GROUP):
        top_ref[h] = jnp.broadcast_to(jnp.max(top_ref[h], axis=1, keepdims=True), (TOK, HD))
    acc_ref[...] = jnp.zeros(acc_ref.shape, f32)
    sum_ref[...] = jnp.zeros(sum_ref.shape, f32)
    for i, n in blocks:
        vals = rows(i, slice(HD, 2 * HD))
        for h in range(GROUP):
            e = jnp.exp2((s_ref[h, :, i * TOK : i * TOK + n] - top_ref[h, :, :n]) * C2)
            sum_ref[h, :, :n] += e
            acc_ref[h] += jnp.dot(e.astype(bf16), vals, preferred_element_type=f32)
    lane = iota((TOK, HD), 1)
    stats = jnp.zeros((TOK, HD), f32)
    for h in range(GROUP):
        out_ref[:, h * HD : (h + 1) * HD] = acc_ref[h]
        stats = jnp.where(lane == h, top_ref[h], stats)
        stats = jnp.where(lane == GROUP + h, jnp.sum(sum_ref[h], axis=1, keepdims=True), stats)
    out_ref[:, GROUP * HD :] = stats


def join_kernel(a_ref, b_ref, out_ref):
    sa, sb = a_ref[:, GROUP * HD :], b_ref[:, GROUP * HD :]
    for h in range(GROUP):
        top_a, top_b = sa[:, h : h + 1], sb[:, h : h + 1]
        top = jnp.maximum(top_a, top_b)
        wa, wb = jnp.exp2((top_a - top) * C2), jnp.exp2((top_b - top) * C2)
        total = sa[:, GROUP + h : GROUP + h + 1] * wa + sb[:, GROUP + h : GROUP + h + 1] * wb
        wa, wb = wa / total, wb / total
        cols = slice(h * HD, (h + 1) * HD)
        out_ref[:, cols] = (a_ref[:, cols] * wa + b_ref[:, cols] * wb).astype(bf16)


VMEM = pl.BlockSpec(memory_space=pltpu.VMEM)
SMEM = pl.BlockSpec(memory_space=pltpu.SMEM)


def swap(x):
    return lax.ppermute(x, "ctx", [(i, i ^ 1) for i in range(NCX)])


def attend(flip, doc_lengths, pos, query, key_value, rest):
    return pl.pallas_call(
        functools.partial(attend_kernel, flip),
        out_shape=jax.ShapeDtypeStruct((TOK, GROUP * HD + HD), f32),
        in_specs=[SMEM, VMEM, VMEM, VMEM, VMEM],
        out_specs=VMEM,
        scratch_shapes=[
            pltpu.VMEM((GROUP, TOK, KEYS + TOK), f32),
            pltpu.VMEM((GROUP, TOK, HD), f32),
            pltpu.VMEM((GROUP, TOK, HD), f32),
            pltpu.VMEM((GROUP, TOK, HD), f32),
        ],
        cost_estimate=pl.CostEstimate(
            flops=4 * GROUP * TOK * KEYS * HD, bytes_accessed=2 * KEYS * HD * 2, transcendentals=GROUP * TOK * KEYS
        ),
        name="attend_partner" if flip else "attend_own",
    )(doc_lengths, pos, query, key_value, rest)


def body(queries, keys, values, counts, doc_lengths):
    slots = NCX * SLOT
    wide = GROUP * HD
    packed, key_value = pl.pallas_call(
        pack_kernel,
        out_shape=(
            jax.ShapeDtypeStruct((slots, wide + HD), bf16),
            jax.ShapeDtypeStruct((MAIN, 2 * HD), bf16),
        ),
        in_specs=[VMEM, VMEM, VMEM, VMEM],
        out_specs=(VMEM, VMEM),
        name="pack",
    )(counts, queries, keys, values)
    got = lax.all_to_all(
        packed.reshape(NCX, SLOT, wide + HD), "ctx", split_axis=0, concat_axis=0, tiled=True
    )
    key_value = lax.all_gather(key_value, "ctx", axis=0, axis_index_groups=SIDES)
    got, key_value = lax.optimization_barrier((got, key_value))
    got = got.reshape(slots, wide + HD)
    pos = pl.pallas_call(
        place_kernel,
        out_shape=jax.ShapeDtypeStruct((NCX + 8, TOK), f32),
        in_specs=[VMEM],
        out_specs=VMEM,
        name="place",
    )(counts)
    query, rest = pl.pallas_call(
        unpack_kernel,
        out_shape=(
            jax.ShapeDtypeStruct((TOK, wide), bf16),
            jax.ShapeDtypeStruct((NCX // 2 * REST, 2 * HD), bf16),
        ),
        in_specs=[VMEM, VMEM],
        out_specs=(VMEM, VMEM),
        name="unpack",
    )(counts, got)
    partner = attend(1, doc_lengths, pos, swap(query), key_value, rest)
    other = swap(partner)
    own = attend(0, doc_lengths, pos, query, key_value, rest)
    return pl.pallas_call(
        join_kernel,
        out_shape=jax.ShapeDtypeStruct((TOK, wide), bf16),
        in_specs=[VMEM, VMEM],
        out_specs=VMEM,
        name="join",
    )(own, other)


def solution(mesh):
    placed = (
        P(("dp", "ctx"), "tp"),
        P(("dp", "ctx"), "tp"),
        P(("dp", "ctx"), "tp"),
        P("dp", None),
        P("dp"),
    )
    return jax.shard_map(
        body, mesh=mesh, in_specs=placed, out_specs=P(("dp", "ctx"), "tp"), check_vma=False
    )
```

profile of v0, /device:TPU:6, one launch (start us, length us, event | category | flops | bytes accessed | tf_op | source)
XLA Modules:
  0.0 133.6 jit_solution(14324762832834848960)
XLA Ops:
  0.0 2.0 %pack.1 = (bf16[256,640]{1,0:T(8,128)(2,1)}, bf16[124,256]{1,0:T(8,128)(2,1)}) custom-call(s32[32,32]{1,0:T(8,128)} %counts_ref.5, bf16[128,512]{1,0:T(8,128)(2,1)} %q_ref.1, bf16[128,128]{1,0:T(8,128)(2,1)} %k_ref.1, bf16[128,128]{1,0:T(8,128)(2,1)} %v_ref.1), custom_call_target="tpu_custom_call" | custom-call | tf_op jit(solution)/shard_map/pack/pallas_call | solution.py:193
  2.0 0.0 copy-start.2
  2.0 28.9 %all-to-all-start = ((bf16[32,8,640]{2,1,0:T(8,128)(2,1)}), bf16[32,8,640]{2,1,0:T(8,128)(2,1)S(1)}, u32[]{:S(2)}, u32[]{:S(2)}) async-start(bf16[32,8,640]{2,1,0:T(8,128)(2,1)} %bitcast.4), calls=%async_computation | async-start | bytes 655360 | tf_op jit(solution)/shard_map/all_to_all | solution.py:203
  30.9 0.0 copy-done.2
  30.9 74.7 %all-gather.1.kv_ref = bf16[16,124,256]{2,1,0:T(8,128)(2,1)} all-gather(bf16[1,124,256]{2,1,0:T(8,128)(2,1)S(1)} %bitcast.5), channel_id=2, replica_groups={{0,16,32,48,64,80,96,112,128,144,160,176,192,208,224,240},{8,24,40,56,7..., dimensions={0}, use_global_device_ids=true | all-gather | bytes 1079296 | tf_op jit(solution)/shard_map/all_gather | solution.py:206
  105.6 0.0 all-to-all-done
  105.6 0.0 copy-start
  105.6 0.7 copy-done
  106.3 1.9 %unpack.1 = (bf16[128,512]{1,0:T(8,128)(2,1)}, bf16[64,256]{1,0:T(8,128)(2,1)}) custom-call(s32[32,32]{1,0:T(8,128)} %counts_ref.5, bf16[256,640]{1,0:T(8,128)(2,1)} %bitcast.3), custom_call_target="tpu_custom_call" | custom-call | tf_op jit(solution)/shard_map/unpack/pallas_call | solution.py:216
  108.2 1.9 %collective-permute-start = (bf16[128,512]{1,0:T(8,128)(2,1)}, bf16[128,512]{1,0:T(8,128)(2,1)S(1)}, u32[]{:S(2)}, u32[]{:S(2)}) collective-permute-start(bf16[128,512]{1,0:T(8,128)(2,1)} %get-tuple-element.14.q_ref), channel_id=1, source_target_pairs={{0,8},{8,0},{16,24},{24,16},{32,40},{40,32},{48,56},{56,48},{64,72... | collective-permute-start | bytes 393224 | tf_op jit(solution)/shard_map/ppermute | solution.py:168
  110.2 2.0 %place.1.pos_ref = f32[40,128]{1,0:T(8,128)} custom-call(s32[32,32]{1,0:T(8,128)} %counts_ref.5), custom_call_target="tpu_custom_call" | custom-call | tf_op jit(solution)/shard_map/place/pallas_call | solution.py:209
  112.2 3.1 %collective-permute-done.q_ref = bf16[128,512]{1,0:T(8,128)(2,1)S(1)} collective-permute-done((bf16[128,512]{1,0:T(8,128)(2,1)}, bf16[128,512]{1,0:T(8,128)(2,1)S(1)}, u32[]{:S(2)}, u32[]{:S(2)}) %collective-permute-start) | collective-permute-done | bytes 131104 | tf_op jit(solution)/shard_map/ppermute | solution.py:168
  115.3 0.0 copy-start.3
  115.3 0.7 copy-done.3
  116.0 5.6 %attend_partner.1 = f32[128,640]{1,0:T(8,128)} custom-call(s32[16]{0:T(128)} %docs_ref.3, f32[40,128]{1,0:T(8,128)} %place.1.pos_ref, bf16[128,512]{1,0:T(8,128)(2,1)} %copy-done.3, bf16[16,124,256]{2,1,0:T(8,128)(2,1)} %all-gather.1.kv_ref, bf16[64,256]{1,0:T(8,128)(2,1)} %get-tuple-element.16.rest_ref), custom_call_target="tpu_custom_call" | custom-call | flops 536870912 | bytes 1048576 | tf_op jit(solution)/shard_map/attend_partner/pallas_call | solution.py:172
  121.6 1.9 %collective-permute-start.1 = (f32[128,640]{1,0:T(8,128)}, f32[128,640]{1,0:T(8,128)S(1)}, u32[]{:S(2)}, u32[]{:S(2)}) collective-permute-start(f32[128,640]{1,0:T(8,128)} %attend_partner.1), channel_id=1, source_target_pairs={{0,8},{8,0},{16,24},{24,16},{32,40},{40,32},{48,56},{56,48},{64,72... | collective-permute-start | bytes 983048 | tf_op jit(solution)/shard_map/ppermute | solution.py:168
  123.5 5.6 %attend_own.1.a_ref = f32[128,640]{1,0:T(8,128)} custom-call(s32[16]{0:T(128)} %docs_ref.3, f32[40,128]{1,0:T(8,128)} %place.1.pos_ref, bf16[128,512]{1,0:T(8,128)(2,1)} %get-tuple-element.14.q_ref, bf16[16,124,256]{2,1,0:T(8,128)(2,1)} %all-gather.1.kv_ref, bf16[64,256]{1,0:T(8,128)(2,1)} %get-tuple-element.16.rest_ref), custom_call_target="tpu_custom_call" | custom-call | flops 536870912 | bytes 1048576 | tf_op jit(solution)/shard_map/attend_own/pallas_call | solution.py:172
  129.1 1.6 %collective-permute-done.1.b_ref = f32[128,640]{1,0:T(8,128)S(1)} collective-permute-done((f32[128,640]{1,0:T(8,128)}, f32[128,640]{1,0:T(8,128)S(1)}, u32[]{:S(2)}, u32[]{:S(2)}) %collective-permute-start.1) | collective-permute-done | bytes 327712 | tf_op jit(solution)/shard_map/ppermute | solution.py:168
  130.7 0.0 copy-start.1
  130.7 0.7 copy-done.1
  131.5 2.1 %join.1 = bf16[128,512]{1,0:T(8,128)(2,1)} custom-call(f32[128,640]{1,0:T(8,128)} %attend_own.1.a_ref, f32[128,640]{1,0:T(8,128)} %copy-done.1), custom_call_target="tpu_custom_call" | custom-call | tf_op jit(solution)/shard_map/join/pallas_call | solution.py:229
Async XLA Ops:
  2.0 28.9 %copy-start.2 = (bf16[124,256]{1,0:T(8,128)(2,1)S(1)}, bf16[124,256]{1,0:T(8,128)(2,1)}, u32[]{:S(2)}) copy-start(bf16[124,256]{1,0:T(8,128)(2,1)} %get-tuple-element.12) | copy-start | bytes 190468
  2.0 103.6 %all-to-all-start = ((bf16[32,8,640]{2,1,0:T(8,128)(2,1)}), bf16[32,8,640]{2,1,0:T(8,128)(2,1)S(1)}, u32[]{:S(2)}, u32[]{:S(2)}) async-start(bf16[32,8,640]{2,1,0:T(8,128)(2,1)} %bitcast.4), calls=%async_computation | async-start | bytes 655360 | tf_op jit(solution)/shard_map/all_to_all | solution.py:203
  105.6 0.7 copy-start
  108.2 7.1 %collective-permute-start = (bf16[128,512]{1,0:T(8,128)(2,1)}, bf16[128,512]{1,0:T(8,128)(2,1)S(1)}, u32[]{:S(2)}, u32[]{:S(2)}) collective-permute-start(bf16[128,512]{1,0:T(8,128)(2,1)} %get-tuple-element.14.q_ref), channel_id=1, source_target_pairs={{0,8},{8,0},{16,24},{24,16},{32,40},{40,32},{48,56},{56,48},{64,72... | collective-permute-start | bytes 393224 | tf_op jit(solution)/shard_map/ppermute | solution.py:168
  115.3 0.7 copy-start.3
  121.6 9.2 %collective-permute-start.1 = (f32[128,640]{1,0:T(8,128)}, f32[128,640]{1,0:T(8,128)S(1)}, u32[]{:S(2)}, u32[]{:S(2)}) collective-permute-start(f32[128,640]{1,0:T(8,128)} %attend_partner.1), channel_id=1, source_target_pairs={{0,8},{8,0},{16,24},{24,16},{32,40},{40,32},{48,56},{56,48},{64,72... | collective-permute-start | bytes 983048 | tf_op jit(solution)/shard_map/ppermute | solution.py:168
  130.7 0.7 copy-start.1
where the time goes:
time: 134 us
  blocking collectives  74.7 us (56%)
  starting transfers between devices  32.7 us (24%)
  Pallas kernels  19.3 us (14%)
  waiting for transfers between devices  4.71 us (4%)
  local copies, waits for them, and re-layouts  2.12 us (2%)
    all_gather x1, blocking collectives, body(): lax.all_gather(key_value, 'ctx', axis=0, axis_index_groups=SIDES)  74.7 us
    all_to_all x1, starting transfers between devices, body(): lax.all_to_all(packed.reshape(NCX, SLOT, wide + HD), 'ctx', split_axis=0,...  28.9 us
    pallas_call x2, Pallas kernels, attend(): pl.pallas_call(functools.partial(attend_kernel, flip), out_shape=jax.Shap...  11.3 us
    ppermute x2, waiting for transfers between devices, swap(): return lax.ppermute(x, 'ctx', [(i, i ^ 1) for i in range(NCX)])  4.71 us
    ppermute x2, starting transfers between devices, swap(): return lax.ppermute(x, 'ctx', [(i, i ^ 1) for i in range(NCX)])  3.82 us
  transfers between devices with their start and end apart: 3, of which 2 were waited for; matrix products, arithmetic and copies ran while one was open for 0% of the time, Pallas kernels for 6%

commit v1 on v0

v1 whole, which is shorter than its diff:
```python
import functools

import jax
import jax.numpy as jnp
from jax import lax
from jax.experimental import pallas as pl
from jax.experimental.pallas import tpu as pltpu
from jax.sharding import PartitionSpec as P

HQ = 32
KVH = 8
HD = 128
GROUP = HQ // KVH
TOK = 128
HALF = 64
NCX = 32
SLOT = 8
SIDE = NCX // 2
KEYS = SIDE * TOK
MAIN = 124
REST = TOK - MAIN
C2 = 1.4426950408889634 / HD**0.5
NEG = -1e30
FAR = 1e9
SIDES = [list(range(0, NCX, 2)), list(range(1, NCX, 2))]

f32 = jnp.float32
bf16 = jnp.bfloat16
i32 = jnp.int32


def iota(shape, dim):
    return lax.broadcasted_iota(i32, shape, dim)


def pack_kernel(counts_ref, q_ref, k_ref, v_ref, out_ref, kv_ref):
    me = lax.axis_index("ctx")
    row = counts_ref[pl.ds(me, 1), :].astype(f32)
    slots = NCX * SLOT
    owner_of = iota((slots, NCX), 0) // SLOT
    owner = iota((slots, NCX), 1)
    start = jnp.sum(jnp.where(owner < owner_of, row, 0.0), axis=1, keepdims=True)
    count = jnp.sum(jnp.where(owner == owner_of, row, 0.0), axis=1, keepdims=True)
    j = iota((slots, 1), 0) % SLOT
    jf = j.astype(f32)
    want = jnp.where(jf < count, start + jf, -1.0)
    lane = iota((slots, TOK), 1)
    pick = jnp.where(lane.astype(f32) == want, 1.0, 0.0).astype(bf16)
    wide = GROUP * HD
    out_ref[:, :wide] = jnp.dot(pick, q_ref[...], preferred_element_type=f32).astype(bf16)
    pick_k = jnp.where(lane == jnp.where(j < REST, MAIN + j, -1), 1.0, 0.0).astype(bf16)
    pick_v = jnp.where(lane == jnp.where(j >= REST, MAIN + j - REST, -1), 1.0, 0.0).astype(bf16)
    rest = jnp.dot(pick_k, k_ref[...], preferred_element_type=f32)
    rest = rest + jnp.dot(pick_v, v_ref[...], preferred_element_type=f32)
    out_ref[:, wide:] = rest.astype(bf16)
    kv_ref[:, :HD] = k_ref[:MAIN, :]
    kv_ref[:, HD:] = v_ref[:MAIN, :]


def place_kernel(counts_ref, kv_ref, rest_ref, pos_ref, all_ref):
    parity = lax.axis_index("ctx") % 2
    counts = counts_ref[...].astype(f32)
    a, b = iota((NCX, NCX), 0), iota((NCX, NCX), 1)
    side = (iota((SIDE, NCX), 1) == 2 * iota((SIDE, NCX), 0) + parity).astype(f32)
    sizes = jnp.dot(side, counts, preferred_element_type=f32)
    starts = jnp.dot(sizes, (a < b).astype(f32), preferred_element_type=f32)
    upto = (b[:SIDE] < 2 * a[:SIDE] + parity).astype(f32)
    before = jnp.dot(upto, counts, preferred_element_type=f32)
    row = iota((SIDE, TOK), 1).astype(f32)
    pos = jnp.zeros((SIDE, TOK), f32)
    for o in range(NCX):
        j = row - starts[:, o : o + 1]
        local = before[:, o : o + 1] + j
        here = jnp.where(local < HALF, local + o * HALF, local + ((2 * NCX - 1 - o) * HALF - HALF))
        pos = jnp.where((j >= 0) & (j < sizes[:, o : o + 1]), here, pos)
    loader, lane = iota((SIDE, TOK), 0), iota((SIDE, TOK), 1)
    rest = jnp.zeros((SIDE, TOK), f32)
    for r in range(REST):
        here = (loader == lane // REST) & (lane % REST == r)
        rest = jnp.where(here, pos[:, MAIN + r : MAIN + r + 1], rest)
    pos_ref[:SIDE, :] = jnp.where(lane < MAIN, pos, FAR)
    rest = jnp.where(lane[:1] < SIDE * REST, jnp.sum(rest, axis=0, keepdims=True), FAR)
    pos_ref[SIDE:, :] = jnp.broadcast_to(rest, (8, TOK))
    for i in range(SIDE):
        all_ref[(i + 1) * TOK - 16 : (i + 1) * TOK, :] = jnp.zeros((16, 2 * HD), bf16)
        all_ref[i * TOK : i * TOK + MAIN, :] = kv_ref[i]
    all_ref[SIDE * TOK : SIDE * TOK + SIDE * REST, :] = rest_ref[...]
    all_ref[SIDE * TOK + SIDE * REST :, :] = jnp.zeros((TOK - SIDE * REST, 2 * HD), bf16)


def unpack_kernel(counts_ref, got_ref, out_ref, rest_ref):
    me = lax.axis_index("ctx")
    slots = NCX * SLOT
    counts = counts_ref[...].astype(f32)
    mine = jnp.sum(jnp.where(iota((NCX, NCX), 1) == me, counts, 0.0), axis=1, keepdims=True)
    src_of, src = iota((NCX, slots), 1) // SLOT, iota((NCX, slots), 0)
    before = jnp.sum(jnp.where(src < src_of, mine, 0.0), axis=0, keepdims=True)
    count = jnp.sum(jnp.where(src == src_of, mine, 0.0), axis=0, keepdims=True)
    j = (iota((1, slots), 1) % SLOT).astype(f32)
    local = jnp.where(j < count, before + j, -1.0)
    pick = jnp.where(iota((TOK, slots), 0).astype(f32) == local, 1.0, 0.0).astype(bf16)
    wide = GROUP * HD
    for h in range(GROUP):
        picked = jnp.dot(pick, got_ref[:, h * HD : (h + 1) * HD], preferred_element_type=f32)
        out_ref[h * TOK : (h + 1) * TOK, :] = picked.astype(bf16)
    n = SIDE * REST
    row, slot = iota((n, slots), 0), iota((n, slots), 1)
    at = (2 * (row // REST) + me % 2) * SLOT + row % REST
    for c in range(2):
        pick = jnp.where(slot == at + c * REST, 1.0, 0.0).astype(bf16)
        rest = jnp.dot(pick, got_ref[:, wide:], preferred_element_type=f32)
        rest_ref[:, c * HD : (c + 1) * HD] = rest.astype(bf16)


def attend_kernel(flip, docs_ref, pos_ref, q_ref, kv_ref, out_ref, s_ref, p_ref, bias_ref):
    me = lax.axis_index("ctx")
    owner = me + flip * (1 - 2 * (me % 2))
    q_id = iota((TOK, HD), 0)
    q_pos = jnp.where(q_id < HALF, owner * HALF + q_id, (2 * NCX - 1 - owner) * HALF + q_id - HALF)
    q_first = jnp.zeros((TOK, HD), i32)
    end = jnp.int32(0)
    for d in range(docs_ref.shape[0]):
        end = end + docs_ref[d]
        q_first = jnp.where(q_pos >= end, end, q_first)
    q_pos, q_first = q_pos.astype(f32), q_first.astype(f32)

    tops = [jnp.full((TOK, HD), NEG, f32) for _ in range(GROUP)]
    for i in range(0, SIDE + 1, 2):
        n = min(2, SIDE + 1 - i)
        for c in range(n):
            k_pos = pos_ref[i + c : i + c + 1, :]
            bias_ref[:, c * TOK : (c + 1) * TOK] = jnp.where((k_pos <= q_pos) & (k_pos >= q_first), 0.0, NEG)
        s = lax.dot_general(
            q_ref[...],
            kv_ref[i * TOK : (i + n) * TOK, :HD],
            (((1,), (1,)), ((), ())),
            preferred_element_type=f32,
        )
        for h in range(GROUP):
            for c in range(n):
                cols = slice(c * TOK, (c + 1) * TOK)
                part = s[h * TOK : (h + 1) * TOK, cols] + bias_ref[:, cols]
                s_ref[h * TOK : (h + 1) * TOK, (i + c) * TOK : (i + c + 1) * TOK] = part
                tops[h] = jnp.maximum(tops[h], part)
    lane = iota((TOK, HD), 1)
    stats = jnp.zeros((TOK, HD), f32)
    totals = []
    for h in range(GROUP):
        top = jnp.broadcast_to(jnp.max(tops[h], axis=1, keepdims=True), (TOK, HD))
        total = jnp.zeros((TOK, HD), f32)
        for i in range(SIDE + 1):
            cols = slice(i * TOK, (i + 1) * TOK)
            e = jnp.exp2((s_ref[h * TOK : (h + 1) * TOK, cols] - top) * C2)
            total = total + e
            p_ref[h * TOK : (h + 1) * TOK, cols] = e.astype(bf16)
        total = jnp.broadcast_to(jnp.sum(total, axis=1, keepdims=True), (TOK, HD))
        totals.append(total)
        for k, value in ((h, top), (GROUP + h, total)):
            if flip:
                for term in range(3):
                    piece = value.astype(bf16).astype(f32)
                    stats = jnp.where(lane == term * 2 * GROUP + k, piece, stats)
                    value = value - piece
            else:
                stats = jnp.where(lane == k, value, stats)
    acc = jnp.dot(p_ref[...], kv_ref[:, HD:], preferred_element_type=f32)
    for h in range(GROUP):
        rows = slice(h * TOK, (h + 1) * TOK)
        out_ref[rows, :] = (acc[rows] / totals[h]).astype(bf16) if flip else acc[rows]
    out_ref[GROUP * TOK :, :] = stats.astype(out_ref.dtype)


def join_kernel(a_ref, b_ref, out_ref):
    sa = a_ref[GROUP * TOK :, :]
    sb = b_ref[GROUP * TOK :, :].astype(f32)

    def stat(k):
        return sum(sb[:, term * 2 * GROUP + k : term * 2 * GROUP + k + 1] for term in range(3))

    for h in range(GROUP):
        top_a, top_b = sa[:, h : h + 1], stat(h)
        top = jnp.maximum(top_a, top_b)
        wa = jnp.exp2((top_a - top) * C2)
        wb = jnp.exp2((top_b - top) * C2) * stat(GROUP + h)
        total = sa[:, GROUP + h : GROUP + h + 1] * wa + wb
        wa, wb = wa / total, wb / total
        rows = slice(h * TOK, (h + 1) * TOK)
        out_ref[:, h * HD : (h + 1) * HD] = (a_ref[rows, :] * wa + b_ref[rows, :].astype(f32) * wb).astype(bf16)


VMEM = pl.BlockSpec(memory_space=pltpu.VMEM)
LIMIT = pltpu.CompilerParams(vmem_limit_bytes=24 * 2**20)
SMEM = pl.BlockSpec(memory_space=pltpu.SMEM)


def near(x):
    return pltpu.with_memory_space_constraint(x, pltpu.VMEM)


def swap(x):
    return lax.ppermute(x, "ctx", [(i, i ^ 1) for i in range(NCX)])


def attend(flip, doc_lengths, pos, query, key_value):
    span = KEYS + TOK
    return pl.pallas_call(
        functools.partial(attend_kernel, flip),
        out_shape=pltpu.VMEM((GROUP * TOK + TOK, HD), bf16 if flip else f32),
        in_specs=[SMEM, VMEM, VMEM, VMEM],
        out_specs=VMEM,
        scratch_shapes=[
            pltpu.VMEM((GROUP * TOK, span), f32),
            pltpu.VMEM((GROUP * TOK, span), bf16),
            pltpu.VMEM((TOK, 2 * TOK), f32),
        ],
        cost_estimate=pl.CostEstimate(
            flops=4 * GROUP * TOK * KEYS * HD, bytes_accessed=2 * KEYS * HD * 2, transcendentals=GROUP * TOK * KEYS
        ),
        compiler_params=LIMIT,
        name="attend_partner" if flip else "attend_own",
    )(doc_lengths, pos, query, key_value)


def body(queries, keys, values, counts, doc_lengths):
    slots = NCX * SLOT
    wide = GROUP * HD
    packed, key_value = pl.pallas_call(
        pack_kernel,
        out_shape=(
            pltpu.VMEM((slots, wide + HD), bf16),
            pltpu.VMEM((MAIN, 2 * HD), bf16),
        ),
        in_specs=[VMEM, VMEM, VMEM, VMEM],
        out_specs=(VMEM, VMEM),
        compiler_params=LIMIT,
        name="pack",
    )(counts, queries, keys, values)
    got = lax.all_to_all(
        packed.reshape(NCX, SLOT, wide + HD), "ctx", split_axis=0, concat_axis=0, tiled=True
    )
    key_value = lax.all_gather(key_value, "ctx", axis=0, axis_index_groups=SIDES)
    got, key_value = lax.optimization_barrier((got, key_value))
    query, rest = pl.pallas_call(
        unpack_kernel,
        out_shape=(
            pltpu.VMEM((GROUP * TOK, HD), bf16),
            pltpu.VMEM((SIDE * REST, 2 * HD), bf16),
        ),
        in_specs=[VMEM, VMEM],
        out_specs=(VMEM, VMEM),
        compiler_params=LIMIT,
        name="unpack",
    )(counts, near(got.reshape(slots, wide + HD)))
    pos, key_value = pl.pallas_call(
        place_kernel,
        out_shape=(
            pltpu.VMEM((SIDE + 8, TOK), f32),
            pltpu.VMEM((KEYS + TOK, 2 * HD), bf16),
        ),
        in_specs=[VMEM, VMEM, VMEM],
        out_specs=(VMEM, VMEM),
        compiler_params=LIMIT,
        name="place",
    )(counts, near(key_value), near(rest))
    pos, query, key_value = near(pos), near(query), near(key_value)
    partner = attend(1, doc_lengths, pos, near(swap(query)), key_value)
    other = swap(partner)
    own = attend(0, doc_lengths, pos, query, key_value)
    return pl.pallas_call(
        join_kernel,
        out_shape=jax.ShapeDtypeStruct((TOK, wide), bf16),
        in_specs=[VMEM, VMEM],
        out_specs=VMEM,
        compiler_params=LIMIT,
        name="join",
    )(near(own), near(other))


def solution(mesh):
    placed = (
        P(("dp", "ctx"), "tp"),
        P(("dp", "ctx"), "tp"),
        P(("dp", "ctx"), "tp"),
        P("dp", None),
        P("dp"),
    )
    return jax.shard_map(
        body, mesh=mesh, in_specs=placed, out_specs=P(("dp", "ctx"), "tp"), check_vma=False
    )
```

time: 134 us -> 126 us (0.940)
  Pallas kernels: 19.3 us -> 11.1 us
  blocking collectives: 74.7 us -> 73 us
    pallas_call x5, Pallas kernels: 17.2 us -> 9.9 us  [the longest x2 7.92 us: attend(): pl.pallas_call(functools.partial(attend_kernel, flip), out_shape=pltpu.VM...]
    all_gather x1, blocking collectives: 74.7 us -> 73 us  [body(): lax.all_gather(key_value, 'ctx', axis=0, axis_index_groups=SIDES)]
    unnamed x8 -> x12, local copies, waits for them, and re-layouts: 2.12 us -> 3.15 us
  transfers between devices with their start and end apart: 3 -> 3, of which waited for: 2 -> 2; matrix products, arithmetic and copies ran while one was open for 0% -> 0% of each run, Pallas kernels for 6% -> 4%
where the time goes in v1:
time: 126 us
  blocking collectives  73 us (58%)
  starting transfers between devices  32.6 us (26%)
  Pallas kernels  11.1 us (9%)
  waiting for transfers between devices  5.73 us (5%)
  local copies, waits for them, and re-layouts  3.15 us (2%)
    all_gather x1, blocking collectives, body(): lax.all_gather(key_value, 'ctx', axis=0, axis_index_groups=SIDES)  73 us
    all_to_all x1, starting transfers between devices, body(): lax.all_to_all(packed.reshape(NCX, SLOT, wide + HD), 'ctx', split_axis=0,...  28.7 us
    pallas_call x2, Pallas kernels, attend(): pl.pallas_call(functools.partial(attend_kernel, flip), out_shape=pltpu.VM...  7.92 us
    ppermute x2, waiting for transfers between devices, swap(): return lax.ppermute(x, 'ctx', [(i, i ^ 1) for i in range(NCX)])  5.73 us
    ppermute x2, starting transfers between devices, swap(): return lax.ppermute(x, 'ctx', [(i, i ^ 1) for i in range(NCX)])  3.84 us
    unnamed x12, local copies, waits for them, and re-layouts  3.15 us
  transfers between devices with their start and end apart: 3, of which 2 were waited for; matrix products, arithmetic and copies ran while one was open for 0% of the time, Pallas kernels for 4%

profile of v1, /device:TPU:6, one launch (start us, length us, event | category | flops | bytes accessed | tf_op | source)
XLA Modules:
  0.0 125.6 jit_solution(5079279305342015317)
XLA Ops:
  0.0 0.0 copy-start
  0.0 0.7 copy-done
  0.7 0.0 copy-start.2
  0.7 0.9 copy-done.2
  1.6 0.0 copy-start.3
  1.6 0.8 copy-done.3
  2.4 0.0 copy-start.4
  2.4 0.8 copy-done.4
  3.1 0.0 copy-start.1
  3.1 1.1 pack.1
  4.2 28.7 %all-to-all-start = ((bf16[32,8,640]{2,1,0:T(8,128)(2,1)}), bf16[32,8,640]{2,1,0:T(8,128)(2,1)S(1)}, u32[]{:S(2)}, u32[]{:S(2)}) async-start(bf16[32,8,640]{2,1,0:T(8,128)(2,1)} %bitcast), calls=%async_computation | async-start | bytes 655360 | tf_op jit(solution)/shard_map/all_to_all | solution.py:238
  33.0 0.0 copy-start.5
  33.0 73.0 %all-gather.1.kv_ref = bf16[16,124,256]{2,1,0:T(8,128)(2,1)S(1)} all-gather(bf16[1,124,256]{2,1,0:T(8,128)(2,1)S(1)} %bitcast.4), channel_id=2, replica_groups={{0,16,32,48,64,80,96,112,128,144,160,176,192,208,224,240},{8,24,40,56,7..., dimensions={0}, use_global_device_ids=true | all-gather | bytes 1079296 | tf_op jit(solution)/shard_map/all_gather | solution.py:241
  106.0 0.0 all-to-all-done
  106.0 0.0 copy-done.1
  106.0 0.3 unpack.1
  106.3 1.9 %collective-permute-start = (bf16[512,128]{1,0:T(8,128)(2,1)S(1)}, bf16[512,128]{1,0:T(8,128)(2,1)S(1)}, u32[]{:S(2)}, u32[]{:S(2)}) collective-permute-start(bf16[512,128]{1,0:T(8,128)(2,1)S(1)} %get-tuple-element.19.q_ref), channel_id=1, source_target_pairs={{0,8},{8,0},{16,24},{24,16},{32,40},{40,32},{48,56},{56,48},{64,72... | collective-permute-start | bytes 393224 | tf_op jit(solution)/shard_map/ppermute | solution.py:201
  108.3 0.6 place.1
  108.8 4.3 %collective-permute-done.q_ref = bf16[512,128]{1,0:T(8,128)(2,1)S(1)} collective-permute-done((bf16[512,128]{1,0:T(8,128)(2,1)S(1)}, bf16[512,128]{1,0:T(8,128)(2,1)S(1)}, u32[]{:S(2)}, u32[]{:S(2)}) %collective-permute-start) | collective-permute-done | bytes 131104 | tf_op jit(solution)/shard_map/ppermute | solution.py:201
  113.2 0.0 copy-done.5
  113.2 4.0 %attend_partner.1 = bf16[640,128]{1,0:T(8,128)(2,1)S(1)} custom-call(s32[16]{0:T(128)S(1)} %copy-done.5, f32[24,128]{1,0:T(8,128)S(1)} %get-tuple-element.18.pos_ref, bf16[512,128]{1,0:T(8,128)(2,1)S(1)} %collective-permute-done.q_ref, bf16[2176,256]{1,0:T(8,128)(2,1)S(1)} %get-tuple-element.20.kv_ref), custom_call_target="tpu_custom_call" | custom-call | flops 536870912 | bytes 1048576 | tf_op jit(solution)/shard_map/attend_partner/pallas_call | solution.py:206
  117.2 1.9 %collective-permute-start.1 = (bf16[640,128]{1,0:T(8,128)(2,1)S(1)}, bf16[640,128]{1,0:T(8,128)(2,1)S(1)}, u32[]{:S(2)}, u32[]{:S(2)}) collective-permute-start(bf16[640,128]{1,0:T(8,128)(2,1)S(1)} %attend_partner.1), channel_id=1, source_target_pairs={{0,8},{8,0},{16,24},{24,16},{32,40},{40,32},{48,56},{56,48},{64,72... | collective-permute-start | bytes 491528 | tf_op jit(solution)/shard_map/ppermute | solution.py:201
  119.2 3.9 %attend_own.1.a_ref = f32[640,128]{1,0:T(8,128)S(1)} custom-call(s32[16]{0:T(128)S(1)} %copy-done.5, f32[24,128]{1,0:T(8,128)S(1)} %get-tuple-element.18.pos_ref, bf16[512,128]{1,0:T(8,128)(2,1)S(1)} %get-tuple-element.19.q_ref, bf16[2176,256]{1,0:T(8,128)(2,1)S(1)} %get-tuple-element.20.kv_ref), custom_call_target="tpu_custom_call" | custom-call | flops 536870912 | bytes 1048576 | tf_op jit(solution)/shard_map/attend_own/pallas_call | solution.py:206
  123.1 1.4 %collective-permute-done.1.b_ref = bf16[640,128]{1,0:T(8,128)(2,1)S(1)} collective-permute-done((bf16[640,128]{1,0:T(8,128)(2,1)S(1)}, bf16[640,128]{1,0:T(8,128)(2,1)S(1)}, u32[]{:S(2)}, u32[]{:S(2)}) %collective-permute-start.1) | collective-permute-done | bytes 163872 | tf_op jit(solution)/shard_map/ppermute | solution.py:201
  124.4 1.2 join.1
Async XLA Ops:
  0.0 0.7 copy-start
  0.7 0.9 copy-start.2
  1.6 0.8 copy-start.3
  2.4 0.8 copy-start.4
  3.1 102.9 %copy-start.1 = (s32[32,32]{1,0:T(8,128)S(1)}, s32[32,32]{1,0:T(8,128)}, u32[]{:S(2)}) copy-start(s32[32,32]{1,0:T(8,128)} %counts_ref.5) | copy-start | bytes 12292
  4.2 101.8 %all-to-all-start = ((bf16[32,8,640]{2,1,0:T(8,128)(2,1)}), bf16[32,8,640]{2,1,0:T(8,128)(2,1)S(1)}, u32[]{:S(2)}, u32[]{:S(2)}) async-start(bf16[32,8,640]{2,1,0:T(8,128)(2,1)} %bitcast), calls=%async_computation | async-start | bytes 655360 | tf_op jit(solution)/shard_map/all_to_all | solution.py:238
  33.0 80.2 %copy-start.5 = (s32[16]{0:T(128)S(1)}, s32[16]{0:T(128)}, u32[]{:S(2)}) copy-start(s32[16]{0:T(128)} %docs_ref.3) | copy-start | bytes 196
  106.3 6.9 %collective-permute-start = (bf16[512,128]{1,0:T(8,128)(2,1)S(1)}, bf16[512,128]{1,0:T(8,128)(2,1)S(1)}, u32[]{:S(2)}, u32[]{:S(2)}) collective-permute-start(bf16[512,128]{1,0:T(8,128)(2,1)S(1)} %get-tuple-element.19.q_ref), channel_id=1, source_target_pairs={{0,8},{8,0},{16,24},{24,16},{32,40},{40,32},{48,56},{56,48},{64,72... | collective-permute-start | bytes 393224 | tf_op jit(solution)/shard_map/ppermute | solution.py:201
  117.2 7.2 %collective-permute-start.1 = (bf16[640,128]{1,0:T(8,128)(2,1)S(1)}, bf16[640,128]{1,0:T(8,128)(2,1)S(1)}, u32[]{:S(2)}, u32[]{:S(2)}) collective-permute-start(bf16[640,128]{1,0:T(8,128)(2,1)S(1)} %attend_partner.1), channel_id=1, source_target_pairs={{0,8},{8,0},{16,24},{24,16},{32,40},{40,32},{48,56},{56,48},{64,72... | collective-permute-start | bytes 491528 | tf_op jit(solution)/shard_map/ppermute | solution.py:201

commit v2 on v1

--- a/solution.py
+++ b/solution.py
@@ -17,8 +17,10 @@
 SLOT = 8
 SIDE = NCX // 2
 KEYS = SIDE * TOK
-MAIN = 124
+MAIN = 127
 REST = TOK - MAIN
+PARTS = 2
+SPAN = SLOT // PARTS * GROUP * HD + HD
 C2 = 1.4426950408889634 / HD**0.5
 NEG = -1e30
 FAR = 1e9
@@ -36,23 +38,20 @@
 def pack_kernel(counts_ref, q_ref, k_ref, v_ref, out_ref, kv_ref):
     me = lax.axis_index("ctx")
     row = counts_ref[pl.ds(me, 1), :].astype(f32)
-    slots = NCX * SLOT
-    owner_of = iota((slots, NCX), 0) // SLOT
-    owner = iota((slots, NCX), 1)
+    n = NCX * PARTS
+    owner_of, owner = iota((n, NCX), 0) // PARTS, iota((n, NCX), 1)
     start = jnp.sum(jnp.where(owner < owner_of, row, 0.0), axis=1, keepdims=True)
     count = jnp.sum(jnp.where(owner == owner_of, row, 0.0), axis=1, keepdims=True)
-    j = iota((slots, 1), 0) % SLOT
-    jf = j.astype(f32)
-    want = jnp.where(jf < count, start + jf, -1.0)
-    lane = iota((slots, TOK), 1)
-    pick = jnp.where(lane.astype(f32) == want, 1.0, 0.0).astype(bf16)
-    wide = GROUP * HD
-    out_ref[:, :wide] = jnp.dot(pick, q_ref[...], preferred_element_type=f32).astype(bf16)
-    pick_k = jnp.where(lane == jnp.where(j < REST, MAIN + j, -1), 1.0, 0.0).astype(bf16)
-    pick_v = jnp.where(lane == jnp.where(j >= REST, MAIN + j - REST, -1), 1.0, 0.0).astype(bf16)
-    rest = jnp.dot(pick_k, k_ref[...], preferred_element_type=f32)
-    rest = rest + jnp.dot(pick_v, v_ref[...], preferred_element_type=f32)
-    out_ref[:, wide:] = rest.astype(bf16)
+    part = iota((n, 1), 0) % PARTS
+    lane = iota((n, TOK), 1).astype(f32)
+    pieces = []
+    for c in range(SLOT // PARTS):
+        j = (part * (SLOT // PARTS) + c).astype(f32)
+        pick = jnp.where(lane == jnp.where(j < count, start + j, -1.0), 1.0, 0.0).astype(bf16)
+        pieces.append(jnp.dot(pick, q_ref[...], preferred_element_type=f32).astype(bf16))
+    last = jnp.where(part == 0, k_ref[MAIN:, :].astype(f32), v_ref[MAIN:, :].astype(f32))
+    pieces.append(last.astype(bf16))
+    out_ref[...] = jnp.concatenate(pieces, axis=1).reshape(NCX, PARTS, SPAN)
     kv_ref[:, :HD] = k_ref[:MAIN, :]
     kv_ref[:, HD:] = v_ref[:MAIN, :]
 
@@ -90,25 +89,27 @@
 
 def unpack_kernel(counts_ref, got_ref, out_ref, rest_ref):
     me = lax.axis_index("ctx")
-    slots = NCX * SLOT
+    n = NCX * PARTS
+    got = got_ref[...].reshape(n, SPAN)
     counts = counts_ref[...].astype(f32)
     mine = jnp.sum(jnp.where(iota((NCX, NCX), 1) == me, counts, 0.0), axis=1, keepdims=True)
-    src_of, src = iota((NCX, slots), 1) // SLOT, iota((NCX, slots), 0)
+    src_of, src = iota((NCX, n), 1) // PARTS, iota((NCX, n), 0)
     before = jnp.sum(jnp.where(src < src_of, mine, 0.0), axis=0, keepdims=True)
     count = jnp.sum(jnp.where(src == src_of, mine, 0.0), axis=0, keepdims=True)
-    j = (iota((1, slots), 1) % SLOT).astype(f32)
-    local = jnp.where(j < count, before + j, -1.0)
-    pick = jnp.where(iota((TOK, slots), 0).astype(f32) == local, 1.0, 0.0).astype(bf16)
+    part = iota((1, n), 1) % PARTS
+    row = iota((TOK, n), 0).astype(f32)
     wide = GROUP * HD
-    for h in range(GROUP):
-        picked = jnp.dot(pick, got_ref[:, h * HD : (h + 1) * HD], preferred_element_type=f32)
-        out_ref[h * TOK : (h + 1) * TOK, :] = picked.astype(bf16)
-    n = SIDE * REST
-    row, slot = iota((n, slots), 0), iota((n, slots), 1)
-    at = (2 * (row // REST) + me % 2) * SLOT + row % REST
-    for c in range(2):
-        pick = jnp.where(slot == at + c * REST, 1.0, 0.0).astype(bf16)
-        rest = jnp.dot(pick, got_ref[:, wide:], preferred_element_type=f32)
+    query = jnp.zeros((TOK, wide), f32)
+    for c in range(SLOT // PARTS):
+        j = (part * (SLOT // PARTS) + c).astype(f32)
+        pick = jnp.where(row == jnp.where(j < count, before + j, -1.0), 1.0, 0.0).astype(bf16)
+        query = query + jnp.dot(pick, got[:, c * wide : (c + 1) * wide], preferred_element_type=f32)
+    for h in range(GROUP):
+        out_ref[h * TOK : (h + 1) * TOK, :] = query[:, h * HD : (h + 1) * HD].astype(bf16)
+    loader, slot = iota((SIDE, n), 0), iota((SIDE, n), 1)
+    for c in range(PARTS):
+        pick = jnp.where(slot == (2 * loader + me % 2) * PARTS + c, 1.0, 0.0).astype(bf16)
+        rest = jnp.dot(pick, got[:, SPAN - HD :], preferred_element_type=f32)
         rest_ref[:, c * HD : (c + 1) * HD] = rest.astype(bf16)
 
 
@@ -222,21 +223,19 @@
 
 
 def body(queries, keys, values, counts, doc_lengths):
-    slots = NCX * SLOT
     wide = GROUP * HD
     packed, key_value = pl.pallas_call(
         pack_kernel,
         out_shape=(
-            pltpu.VMEM((slots, wide + HD), bf16),
+            pltpu.VMEM((NCX, PARTS, SPAN), bf16),
             pltpu.VMEM((MAIN, 2 * HD), bf16),
         ),
         in_specs=[VMEM, VMEM, VMEM, VMEM],
         out_specs=(VMEM, VMEM),
-        compiler_params=LIMIT,
         name="pack",
     )(counts, queries, keys, values)
     got = lax.all_to_all(
-        packed.reshape(NCX, SLOT, wide + HD), "ctx", split_axis=0, concat_axis=0, tiled=True
+        packed, "ctx", split_axis=0, concat_axis=0, tiled=True
     )
     key_value = lax.all_gather(key_value, "ctx", axis=0, axis_index_groups=SIDES)
     got, key_value = lax.optimization_barrier((got, key_value))
@@ -250,7 +249,7 @@
         out_specs=(VMEM, VMEM),
         compiler_params=LIMIT,
         name="unpack",
-    )(counts, near(got.reshape(slots, wide + HD)))
+    )(counts, near(got))
     pos, key_value = pl.pallas_call(
         place_kernel,
         out_shape=(

time: 126 us -> 120 us (0.952)
  blocking collectives: 73 us -> 68.4 us
  local copies, waits for them, and re-layouts: 3.15 us -> 0.01 us
    all_gather x1, blocking collectives: 73 us -> 68.4 us  [body(): lax.all_gather(key_value, 'ctx', axis=0, axis_index_groups=SIDES)]
    unnamed x12 -> x4, local copies, waits for them, and re-layouts: 3.15 us -> 0.01 us
where the time goes in v2:
time: 120 us; the launch traced here: 119 us
  blocking collectives  68.4 us (57%)
  starting transfers between devices  32.6 us (27%)
  Pallas kernels  12 us (10%)
  waiting for transfers between devices  5.74 us (5%)
    all_gather x1, blocking collectives, body(): lax.all_gather(key_value, 'ctx', axis=0, axis_index_groups=SIDES)  68.4 us
    all_to_all x1, starting transfers between devices, body(): got = lax.all_to_all(packed, 'ctx', split_axis=0, concat_axis=0, tiled=True)  28.7 us
    pallas_call x2, Pallas kernels, attend(): pl.pallas_call(functools.partial(attend_kernel, flip), out_shape=pltpu.VM...  7.93 us
    ppermute x2, waiting for transfers between devices, swap(): return lax.ppermute(x, 'ctx', [(i, i ^ 1) for i in range(NCX)])  5.74 us
    ppermute x2, starting transfers between devices, swap(): return lax.ppermute(x, 'ctx', [(i, i ^ 1) for i in range(NCX)])  3.84 us
  transfers between devices with their start and end apart: 3, of which 2 were waited for; matrix products, arithmetic and copies ran while one was open for 0% of the time, Pallas kernels for 4%

profile of v2, /device:TPU:6, one launch (start us, length us, event | category | flops | bytes accessed | tf_op | source)
XLA Modules:
  0.0 118.8 jit_solution(17298431898555072629)
XLA Ops:
  0.0 0.0 copy-start
  0.0 2.0 %pack.1 = (bf16[32,2,2176]{2,1,0:T(2,128)(2,1)}, bf16[127,256]{1,0:T(8,128)(2,1)S(1)}) custom-call(s32[32,32]{1,0:T(8,128)} %counts_ref.5, bf16[128,512]{1,0:T(8,128)(2,1)} %q_ref.1, bf16[128,128]{1,0:T(8,128)(2,1)} %k_ref.1, bf16[128,128]{1,0:T(8,128)(2,1)} %v_ref.1), custom_call_target="tpu_custom_call" | custom-call | tf_op jit(solution)/shard_map/pack/pallas_call | solution.py:227
  2.0 28.7 %all-to-all-start = ((bf16[32,2,2176]{2,1,0:T(2,128)(2,1)}), bf16[32,2,2176]{2,1,0:T(2,128)(2,1)S(1)}, u32[]{:S(2)}, u32[]{:S(2)}) async-start(bf16[32,2,2176]{2,1,0:T(2,128)(2,1)} %get-tuple-element.13), calls=%async_computation | async-start | bytes 557056 | tf_op jit(solution)/shard_map/all_to_all | solution.py:237
  30.7 0.0 copy-start.1
  30.7 68.4 %all-gather.1.kv_ref = bf16[16,127,256]{2,1,0:T(8,128)(2,1)S(1)} all-gather(bf16[1,127,256]{2,1,0:T(8,128)(2,1)S(1)} %bitcast.1), channel_id=2, replica_groups={{0,16,32,48,64,80,96,112,128,144,160,176,192,208,224,240},{8,24,40,56,7..., dimensions={0}, use_global_device_ids=true | all-gather | bytes 1105408 | tf_op jit(solution)/shard_map/all_gather | solution.py:240
  99.1 0.0 all-to-all-done.got_ref
  99.1 0.0 copy-done
  99.1 0.4 unpack.1
  99.5 1.9 %collective-permute-start = (bf16[512,128]{1,0:T(8,128)(2,1)S(1)}, bf16[512,128]{1,0:T(8,128)(2,1)S(1)}, u32[]{:S(2)}, u32[]{:S(2)}) collective-permute-start(bf16[512,128]{1,0:T(8,128)(2,1)S(1)} %get-tuple-element.19.q_ref), channel_id=1, source_target_pairs={{0,8},{8,0},{16,24},{24,16},{32,40},{40,32},{48,56},{56,48},{64,72... | collective-permute-start | bytes 393224 | tf_op jit(solution)/shard_map/ppermute | solution.py:202
  101.5 0.6 place.1
  102.0 4.4 %collective-permute-done.q_ref = bf16[512,128]{1,0:T(8,128)(2,1)S(1)} collective-permute-done((bf16[512,128]{1,0:T(8,128)(2,1)S(1)}, bf16[512,128]{1,0:T(8,128)(2,1)S(1)}, u32[]{:S(2)}, u32[]{:S(2)}) %collective-permute-start) | collective-permute-done | bytes 131104 | tf_op jit(solution)/shard_map/ppermute | solution.py:202
  106.4 0.0 copy-done.1
  106.4 4.0 %attend_partner.1 = bf16[640,128]{1,0:T(8,128)(2,1)S(1)} custom-call(s32[16]{0:T(128)S(1)} %copy-done.1, f32[24,128]{1,0:T(8,128)S(1)} %get-tuple-element.18.pos_ref, bf16[512,128]{1,0:T(8,128)(2,1)S(1)} %collective-permute-done.q_ref, bf16[2176,256]{1,0:T(8,128)(2,1)S(1)} %get-tuple-element.20.kv_ref), custom_call_target="tpu_custom_call" | custom-call | flops 536870912 | bytes 1048576 | tf_op jit(solution)/shard_map/attend_partner/pallas_call | solution.py:207
  110.4 1.9 %collective-permute-start.1 = (bf16[640,128]{1,0:T(8,128)(2,1)S(1)}, bf16[640,128]{1,0:T(8,128)(2,1)S(1)}, u32[]{:S(2)}, u32[]{:S(2)}) collective-permute-start(bf16[640,128]{1,0:T(8,128)(2,1)S(1)} %attend_partner.1), channel_id=1, source_target_pairs={{0,8},{8,0},{16,24},{24,16},{32,40},{40,32},{48,56},{56,48},{64,72... | collective-permute-start | bytes 491528 | tf_op jit(solution)/shard_map/ppermute | solution.py:202
  112.4 3.9 %attend_own.1.a_ref = f32[640,128]{1,0:T(8,128)S(1)} custom-call(s32[16]{0:T(128)S(1)} %copy-done.1, f32[24,128]{1,0:T(8,128)S(1)} %get-tuple-element.18.pos_ref, bf16[512,128]{1,0:T(8,128)(2,1)S(1)} %get-tuple-element.19.q_ref, bf16[2176,256]{1,0:T(8,128)(2,1)S(1)} %get-tuple-element.20.kv_ref), custom_call_target="tpu_custom_call" | custom-call | flops 536870912 | bytes 1048576 | tf_op jit(solution)/shard_map/attend_own/pallas_call | solution.py:207
  116.3 1.4 %collective-permute-done.1.b_ref = bf16[640,128]{1,0:T(8,128)(2,1)S(1)} collective-permute-done((bf16[640,128]{1,0:T(8,128)(2,1)S(1)}, bf16[640,128]{1,0:T(8,128)(2,1)S(1)}, u32[]{:S(2)}, u32[]{:S(2)}) %collective-permute-start.1) | collective-permute-done | bytes 163872 | tf_op jit(solution)/shard_map/ppermute | solution.py:202
  117.6 1.2 join.1
Async XLA Ops:
  0.0 99.1 %copy-start = (s32[32,32]{1,0:T(8,128)S(1)}, s32[32,32]{1,0:T(8,128)}, u32[]{:S(2)}) copy-start(s32[32,32]{1,0:T(8,128)} %counts_ref.5) | copy-start | bytes 12292
  2.0 97.2 %all-to-all-start = ((bf16[32,2,2176]{2,1,0:T(2,128)(2,1)}), bf16[32,2,2176]{2,1,0:T(2,128)(2,1)S(1)}, u32[]{:S(2)}, u32[]{:S(2)}) async-start(bf16[32,2,2176]{2,1,0:T(2,128)(2,1)} %get-tuple-element.13), calls=%async_computation | async-start | bytes 557056 | tf_op jit(solution)/shard_map/all_to_all | solution.py:237
  30.7 75.7 %copy-start.1 = (s32[16]{0:T(128)S(1)}, s32[16]{0:T(128)}, u32[]{:S(2)}) copy-start(s32[16]{0:T(128)} %docs_ref.3) | copy-start | bytes 196
  99.5 6.9 %collective-permute-start = (bf16[512,128]{1,0:T(8,128)(2,1)S(1)}, bf16[512,128]{1,0:T(8,128)(2,1)S(1)}, u32[]{:S(2)}, u32[]{:S(2)}) collective-permute-start(bf16[512,128]{1,0:T(8,128)(2,1)S(1)} %get-tuple-element.19.q_ref), channel_id=1, source_target_pairs={{0,8},{8,0},{16,24},{24,16},{32,40},{40,32},{48,56},{56,48},{64,72... | collective-permute-start | bytes 393224 | tf_op jit(solution)/shard_map/ppermute | solution.py:202
  110.4 7.2 %collective-permute-start.1 = (bf16[640,128]{1,0:T(8,128)(2,1)S(1)}, bf16[640,128]{1,0:T(8,128)(2,1)S(1)}, u32[]{:S(2)}, u32[]{:S(2)}) collective-permute-start(bf16[640,128]{1,0:T(8,128)(2,1)S(1)} %attend_partner.1), channel_id=1, source_target_pairs={{0,8},{8,0},{16,24},{24,16},{32,40},{40,32},{48,56},{56,48},{64,72... | collective-permute-start | bytes 491528 | tf_op jit(solution)/shard_map/ppermute | solution.py:202

commit v3 on v2

--- a/solution.py
+++ b/solution.py
@@ -23,6 +23,7 @@
 SPAN = SLOT // PARTS * GROUP * HD + HD
 C2 = 1.4426950408889634 / HD**0.5
 NEG = -1e30
+STEP = 4
 FAR = 1e9
 SIDES = [list(range(0, NCX, 2)), list(range(1, NCX, 2))]
 
@@ -56,8 +57,9 @@
     kv_ref[:, HD:] = v_ref[:MAIN, :]
 
 
-def place_kernel(counts_ref, kv_ref, rest_ref, pos_ref, all_ref):
-    parity = lax.axis_index("ctx") % 2
+def place_kernel(docs_ref, counts_ref, kv_ref, rest_ref, bias_ref, all_ref):
+    me = lax.axis_index("ctx")
+    parity = me % 2
     counts = counts_ref[...].astype(f32)
     a, b = iota((NCX, NCX), 0), iota((NCX, NCX), 1)
     side = (iota((SIDE, NCX), 1) == 2 * iota((SIDE, NCX), 0) + parity).astype(f32)
@@ -77,9 +79,22 @@
     for r in range(REST):
         here = (loader == lane // REST) & (lane % REST == r)
         rest = jnp.where(here, pos[:, MAIN + r : MAIN + r + 1], rest)
-    pos_ref[:SIDE, :] = jnp.where(lane < MAIN, pos, FAR)
+    pos = jnp.where(lane < MAIN, pos, FAR)
     rest = jnp.where(lane[:1] < SIDE * REST, jnp.sum(rest, axis=0, keepdims=True), FAR)
-    pos_ref[SIDE:, :] = jnp.broadcast_to(rest, (8, TOK))
+    for flip in range(2):
+        owner = me + flip * (1 - 2 * parity)
+        q_id = iota((TOK, HD), 0)
+        q_pos = jnp.where(q_id < HALF, owner * HALF + q_id, (2 * NCX - 1 - owner) * HALF + q_id - HALF)
+        q_first = jnp.zeros((TOK, HD), i32)
+        end = jnp.int32(0)
+        for d in range(docs_ref.shape[0]):
+            end = end + docs_ref[d]
+            q_first = jnp.where(q_pos >= end, end, q_first)
+        q_pos, q_first = q_pos.astype(f32), q_first.astype(f32)
+        for i in range(SIDE + 1):
+            k_pos = pos[i : i + 1, :] if i < SIDE else rest
+            seen = jnp.where((k_pos <= q_pos) & (k_pos >= q_first), 0.0, NEG)
+            bias_ref[flip, i // 2, :, i % 2 * TOK : (i % 2 + 1) * TOK] = seen
     for i in range(SIDE):
         all_ref[(i + 1) * TOK - 16 : (i + 1) * TOK, :] = jnp.zeros((16, 2 * HD), bf16)
         all_ref[i * TOK : i * TOK + MAIN, :] = kv_ref[i]
@@ -113,61 +128,77 @@
         rest_ref[:, c * HD : (c + 1) * HD] = rest.astype(bf16)
 
 
-def attend_kernel(flip, docs_ref, pos_ref, q_ref, kv_ref, out_ref, s_ref, p_ref, bias_ref):
-    me = lax.axis_index("ctx")
-    owner = me + flip * (1 - 2 * (me % 2))
-    q_id = iota((TOK, HD), 0)
-    q_pos = jnp.where(q_id < HALF, owner * HALF + q_id, (2 * NCX - 1 - owner) * HALF + q_id - HALF)
-    q_first = jnp.zeros((TOK, HD), i32)
-    end = jnp.int32(0)
-    for d in range(docs_ref.shape[0]):
-        end = end + docs_ref[d]
-        q_first = jnp.where(q_pos >= end, end, q_first)
-    q_pos, q_first = q_pos.astype(f32), q_first.astype(f32)
-
-    tops = [jnp.full((TOK, HD), NEG, f32) for _ in range(GROUP)]
-    for i in range(0, SIDE + 1, 2):
-        n = min(2, SIDE + 1 - i)
-        for c in range(n):
-            k_pos = pos_ref[i + c : i + c + 1, :]
-            bias_ref[:, c * TOK : (c + 1) * TOK] = jnp.where((k_pos <= q_pos) & (k_pos >= q_first), 0.0, NEG)
+def attend_kernel(flip, bias_ref, q_ref, kv_ref, out_ref, s_ref, top_ref, sum_ref, acc_ref):
+    two = 2 * TOK
+
+    def scores(pair, i, n):
         s = lax.dot_general(
-            q_ref[...],
-            kv_ref[i * TOK : (i + n) * TOK, :HD],
+            q_ref[pair * two : (pair + 1) * two, :],
+            kv_ref[pl.ds(i * two, n), :HD],
             (((1,), (1,)), ((), ())),
             preferred_element_type=f32,
         )
-        for h in range(GROUP):
-            for c in range(n):
-                cols = slice(c * TOK, (c + 1) * TOK)
-                part = s[h * TOK : (h + 1) * TOK, cols] + bias_ref[:, cols]
-                s_ref[h * TOK : (h + 1) * TOK, (i + c) * TOK : (i + c + 1) * TOK] = part
-                tops[h] = jnp.maximum(tops[h], part)
+        for h in range(2):
+            top = top_ref[2 * pair + h]
+            for c in range(0, n, TOK):
+                part = s[h * TOK : (h + 1) * TOK, c : c + TOK] + bias_ref[flip, i, :, c : c + TOK]
+                s_ref[pair, i, h * TOK : (h + 1) * TOK, c : c + TOK] = part
+                top = jnp.maximum(top, part)
+            top_ref[2 * pair + h] = top
+
+    def weights(pair, i, n):
+        rows = []
+        for h in range(2):
+            top = top_ref[2 * pair + h]
+            total = sum_ref[2 * pair + h]
+            cols = []
+            for c in range(0, n, TOK):
+                e = jnp.exp2((s_ref[pair, i, h * TOK : (h + 1) * TOK, c : c + TOK] - top) * C2)
+                total = total + e
+                cols.append(e.astype(bf16))
+            sum_ref[2 * pair + h] = total
+            rows.append(jnp.concatenate(cols, axis=1))
+        weight = jnp.concatenate(rows, axis=0)
+        acc_ref[pair] += jnp.dot(weight, kv_ref[pl.ds(i * two, n), HD:], preferred_element_type=f32)
+
+    def sweep(*steps):
+        def trip(t, carry):
+            for k in range(STEP):
+                for step, pair in steps:
+                    step(pair, t * STEP + k, two)
+            return carry
+
+        lax.fori_loop(0, SIDE // 2 // STEP, trip, 0)
+        for step, pair in steps:
+            step(pair, SIDE // 2, TOK)
+
+    def settle(pair):
+        for h in range(2 * pair, 2 * pair + 2):
+            top_ref[h] = jnp.broadcast_to(jnp.max(top_ref[h], axis=1, keepdims=True), (TOK, HD))
+
+    top_ref[...] = jnp.full(top_ref.shape, NEG, f32)
+    sum_ref[...] = jnp.zeros(sum_ref.shape, f32)
+    acc_ref[...] = jnp.zeros(acc_ref.shape, f32)
+    sweep((scores, 0))
+    settle(0)
+    sweep((scores, 1), (weights, 0))
+    settle(1)
+    sweep((weights, 1))
     lane = iota((TOK, HD), 1)
     stats = jnp.zeros((TOK, HD), f32)
-    totals = []
     for h in range(GROUP):
-        top = jnp.broadcast_to(jnp.max(tops[h], axis=1, keepdims=True), (TOK, HD))
-        total = jnp.zeros((TOK, HD), f32)
-        for i in range(SIDE + 1):
-            cols = slice(i * TOK, (i + 1) * TOK)
-            e = jnp.exp2((s_ref[h * TOK : (h + 1) * TOK, cols] - top) * C2)
-            total = total + e
-            p_ref[h * TOK : (h + 1) * TOK, cols] = e.astype(bf16)
-        total = jnp.broadcast_to(jnp.sum(total, axis=1, keepdims=True), (TOK, HD))
-        totals.append(total)
-        for k, value in ((h, top), (GROUP + h, total)):
-            if flip:
-                for term in range(3):
-                    piece = value.astype(bf16).astype(f32)
-                    stats = jnp.where(lane == term * 2 * GROUP + k, piece, stats)
-                    value = value - piece
-            else:
-                stats = jnp.where(lane == k, value, stats)
-    acc = jnp.dot(p_ref[...], kv_ref[:, HD:], preferred_element_type=f32)
-    for h in range(GROUP):
-        rows = slice(h * TOK, (h + 1) * TOK)
-        out_ref[rows, :] = (acc[rows] / totals[h]).astype(bf16) if flip else acc[rows]
+        total = jnp.broadcast_to(jnp.sum(sum_ref[h], axis=1, keepdims=True), (TOK, HD))
+        stats = jnp.where(lane == h, top_ref[h], stats)
+        stats = jnp.where(lane == GROUP + h, total, stats)
+        acc = acc_ref[h // 2, h % 2 * TOK : (h % 2 + 1) * TOK, :]
+        out_ref[h * TOK : (h + 1) * TOK, :] = (acc / total).astype(bf16) if flip else acc
+    if flip:
+        terms = jnp.zeros((TOK, HD), f32)
+        for term in range(3):
+            piece = stats.astype(bf16).astype(f32)
+            terms = terms + (pltpu.roll(piece, term * 2 * GROUP, axis=1) if term else piece)
+            stats = stats - piece
+        stats = terms
     out_ref[GROUP * TOK :, :] = stats.astype(out_ref.dtype)
 
 
@@ -202,24 +233,24 @@
     return lax.ppermute(x, "ctx", [(i, i ^ 1) for i in range(NCX)])
 
 
-def attend(flip, doc_lengths, pos, query, key_value):
-    span = KEYS + TOK
+def attend(flip, bias, query, key_value):
     return pl.pallas_call(
         functools.partial(attend_kernel, flip),
         out_shape=pltpu.VMEM((GROUP * TOK + TOK, HD), bf16 if flip else f32),
-        in_specs=[SMEM, VMEM, VMEM, VMEM],
+        in_specs=[VMEM, VMEM, VMEM],
         out_specs=VMEM,
         scratch_shapes=[
-            pltpu.VMEM((GROUP * TOK, span), f32),
-            pltpu.VMEM((GROUP * TOK, span), bf16),
-            pltpu.VMEM((TOK, 2 * TOK), f32),
+            pltpu.VMEM((2, SIDE // 2 + 1, 2 * TOK, 2 * TOK), f32),
+            pltpu.VMEM((GROUP, TOK, HD), f32),
+            pltpu.VMEM((GROUP, TOK, HD), f32),
+            pltpu.VMEM((2, 2 * TOK, HD), f32),
         ],
         cost_estimate=pl.CostEstimate(
             flops=4 * GROUP * TOK * KEYS * HD, bytes_accessed=2 * KEYS * HD * 2, transcendentals=GROUP * TOK * KEYS
         ),
         compiler_params=LIMIT,
         name="attend_partner" if flip else "attend_own",
-    )(doc_lengths, pos, query, key_value)
+    )(bias, query, key_value)
 
 
 def body(queries, keys, values, counts, doc_lengths):
@@ -250,21 +281,21 @@
         compiler_params=LIMIT,
         name="unpack",
     )(counts, near(got))
-    pos, key_value = pl.pallas_call(
+    bias, key_value = pl.pallas_call(
         place_kernel,
         out_shape=(
-            pltpu.VMEM((SIDE + 8, TOK), f32),
+            pltpu.VMEM((2, SIDE // 2 + 1, TOK, 2 * TOK), f32),
             pltpu.VMEM((KEYS + TOK, 2 * HD), bf16),
         ),
-        in_specs=[VMEM, VMEM, VMEM],
+        in_specs=[SMEM, VMEM, VMEM, VMEM],
         out_specs=(VMEM, VMEM),
         compiler_params=LIMIT,
         name="place",
-    )(counts, near(key_value), near(rest))
-    pos, query, key_value = near(pos), near(query), near(key_value)
-    partner = attend(1, doc_lengths, pos, near(swap(query)), key_value)
+    )(doc_lengths, counts, near(key_value), near(rest))
+    bias, query, key_value = near(bias), near(query), near(key_value)
+    partner = attend(1, bias, near(swap(query)), key_value)
     other = swap(partner)
-    own = attend(0, doc_lengths, pos, query, key_value)
+    own = attend(0, bias, query, key_value)
     return pl.pallas_call(
         join_kernel,
         out_shape=jax.ShapeDtypeStruct((TOK, wide), bf16),

time: 120 us -> 120 us (level)
  the two profiles are of different devices: /device:TPU:6 before, /device:TPU:138 now
where the time goes in v3:
time: 120 us
  blocking collectives  70.3 us (59%)
  starting transfers between devices  31.1 us (26%)
  Pallas kernels  10.9 us (9%)
  waiting for transfers between devices  6.3 us (5%)
  local copies, waits for them, and re-layouts  1.37 us (1%)
    all_gather x1, blocking collectives, body(): lax.all_gather(key_value, 'ctx', axis=0, axis_index_groups=SIDES)  70.3 us
    all_to_all x1, starting transfers between devices, body(): got = lax.all_to_all(packed, 'ctx', split_axis=0, concat_axis=0, tiled=True)  27.2 us
    ppermute x2, waiting for transfers between devices, swap(): return lax.ppermute(x, 'ctx', [(i, i ^ 1) for i in range(NCX)])  6.29 us
    pallas_call x2, Pallas kernels, attend(): pl.pallas_call(functools.partial(attend_kernel, flip), out_shape=pltpu.VM...  5.95 us
    ppermute x2, starting transfers between devices, swap(): return lax.ppermute(x, 'ctx', [(i, i ^ 1) for i in range(NCX)])  3.84 us
  transfers between devices with their start and end apart: 3, of which 2 were waited for; matrix products, arithmetic and copies ran while one was open for 0% of the time, Pallas kernels for 4%

profile of v3, /device:TPU:138, one launch (start us, length us, event | category | flops | bytes accessed | tf_op | source)
XLA Modules:
  0.0 120.0 jit_solution(14639215283051567012)
XLA Ops:
  0.0 1.9 %pack.1 = (bf16[32,2,2176]{2,1,0:T(2,128)(2,1)}, bf16[127,256]{1,0:T(8,128)(2,1)S(1)}) custom-call(s32[32,32]{1,0:T(8,128)} %counts_ref.5, bf16[128,512]{1,0:T(8,128)(2,1)} %q_ref.1, bf16[128,128]{1,0:T(8,128)(2,1)} %k_ref.1, bf16[128,128]{1,0:T(8,128)(2,1)} %v_ref.1), custom_call_target="tpu_custom_call" | custom-call | tf_op jit(solution)/shard_map/pack/pallas_call | solution.py:258
  1.9 27.2 %all-to-all-start = ((bf16[32,2,2176]{2,1,0:T(2,128)(2,1)}), bf16[32,2,2176]{2,1,0:T(2,128)(2,1)S(1)}, u32[]{:S(2)}, u32[]{:S(2)}) async-start(bf16[32,2,2176]{2,1,0:T(2,128)(2,1)} %get-tuple-element.13), calls=%async_computation | async-start | bytes 557056 | tf_op jit(solution)/shard_map/all_to_all | solution.py:268
  29.2 70.3 %all-gather.1.kv_ref = bf16[16,127,256]{2,1,0:T(8,128)(2,1)S(1)} all-gather(bf16[1,127,256]{2,1,0:T(8,128)(2,1)S(1)} %bitcast.1), channel_id=2, replica_groups={{0,16,32,48,64,80,96,112,128,144,160,176,192,208,224,240},{8,24,40,56,7..., dimensions={0}, use_global_device_ids=true | all-gather | bytes 1105408 | tf_op jit(solution)/shard_map/all_gather | solution.py:271
  99.5 0.0 all-to-all-done.got_ref
  99.5 0.0 copy-start
  99.5 0.7 copy-done
  100.2 0.4 unpack.1
  100.6 1.9 %collective-permute-start = (bf16[512,128]{1,0:T(8,128)(2,1)S(1)}, bf16[512,128]{1,0:T(8,128)(2,1)S(1)}, u32[]{:S(2)}, u32[]{:S(2)}) collective-permute-start(bf16[512,128]{1,0:T(8,128)(2,1)S(1)} %get-tuple-element.19.q_ref), channel_id=1, source_target_pairs={{0,8},{8,0},{16,24},{24,16},{32,40},{40,32},{48,56},{56,48},{64,72... | collective-permute-start | bytes 393224 | tf_op jit(solution)/shard_map/ppermute | solution.py:233
  102.6 0.0 copy-start.1
  102.6 0.6 copy-done.1
  103.2 1.5 %place.1 = (f32[2,9,128,256]{3,2,1,0:T(8,128)S(1)}, bf16[2176,256]{1,0:T(8,128)(2,1)S(1)}) custom-call(s32[16]{0:T(128)S(1)} %copy-done.1, s32[32,32]{1,0:T(8,128)S(1)} %copy-done, bf16[16,127,256]{2,1,0:T(8,128)(2,1)S(1)} %all-gather.1.kv_ref, bf16[16,256]{1,0:T(8,128)(2,1)S(1)} %get-tuple-element.17.rest_ref), custom_call_target="tpu_custom_call" | custom-call | tf_op jit(solution)/shard_map/place/pallas_call | solution.py:284
  104.7 4.0 %collective-permute-done.q_ref = bf16[512,128]{1,0:T(8,128)(2,1)S(1)} collective-permute-done((bf16[512,128]{1,0:T(8,128)(2,1)S(1)}, bf16[512,128]{1,0:T(8,128)(2,1)S(1)}, u32[]{:S(2)}, u32[]{:S(2)}) %collective-permute-start) | collective-permute-done | bytes 131104 | tf_op jit(solution)/shard_map/ppermute | solution.py:233
  108.6 3.0 %attend_partner.1 = bf16[640,128]{1,0:T(8,128)(2,1)S(1)} custom-call(f32[2,9,128,256]{3,2,1,0:T(8,128)S(1)} %get-tuple-element.18.bias_ref, bf16[512,128]{1,0:T(8,128)(2,1)S(1)} %collective-permute-done.q_ref, bf16[2176,256]{1,0:T(8,128)(2,1)S(1)} %get-tuple-element.20.kv_ref), custom_call_target="tpu_custom_call" | custom-call | flops 536870912 | bytes 1048576 | tf_op jit(solution)/shard_map/attend_partner/pallas_call | solution.py:237
  111.7 1.9 %collective-permute-start.1 = (bf16[640,128]{1,0:T(8,128)(2,1)S(1)}, bf16[640,128]{1,0:T(8,128)(2,1)S(1)}, u32[]{:S(2)}, u32[]{:S(2)}) collective-permute-start(bf16[640,128]{1,0:T(8,128)(2,1)S(1)} %attend_partner.1), channel_id=1, source_target_pairs={{0,8},{8,0},{16,24},{24,16},{32,40},{40,32},{48,56},{56,48},{64,72... | collective-permute-start | bytes 491528 | tf_op jit(solution)/shard_map/ppermute | solution.py:233
  113.6 2.9 %attend_own.1.a_ref = f32[640,128]{1,0:T(8,128)S(1)} custom-call(f32[2,9,128,256]{3,2,1,0:T(8,128)S(1)} %get-tuple-element.18.bias_ref, bf16[512,128]{1,0:T(8,128)(2,1)S(1)} %get-tuple-element.19.q_ref, bf16[2176,256]{1,0:T(8,128)(2,1)S(1)} %get-tuple-element.20.kv_ref), custom_call_target="tpu_custom_call" | custom-call | flops 536870912 | bytes 1048576 | tf_op jit(solution)/shard_map/attend_own/pallas_call | solution.py:237
  116.5 2.3 %collective-permute-done.1.b_ref = bf16[640,128]{1,0:T(8,128)(2,1)S(1)} collective-permute-done((bf16[640,128]{1,0:T(8,128)(2,1)S(1)}, bf16[640,128]{1,0:T(8,128)(2,1)S(1)}, u32[]{:S(2)}, u32[]{:S(2)}) %collective-permute-start.1) | collective-permute-done | bytes 163872 | tf_op jit(solution)/shard_map/ppermute | solution.py:233
  118.9 1.2 join.1
Async XLA Ops:
  1.9 97.6 %all-to-all-start = ((bf16[32,2,2176]{2,1,0:T(2,128)(2,1)}), bf16[32,2,2176]{2,1,0:T(2,128)(2,1)S(1)}, u32[]{:S(2)}, u32[]{:S(2)}) async-start(bf16[32,2,2176]{2,1,0:T(2,128)(2,1)} %get-tuple-element.13), calls=%async_computation | async-start | bytes 557056 | tf_op jit(solution)/shard_map/all_to_all | solution.py:268
  99.5 0.7 copy-start
  100.6 8.0 %collective-permute-start = (bf16[512,128]{1,0:T(8,128)(2,1)S(1)}, bf16[512,128]{1,0:T(8,128)(2,1)S(1)}, u32[]{:S(2)}, u32[]{:S(2)}) collective-permute-start(bf16[512,128]{1,0:T(8,128)(2,1)S(1)} %get-tuple-element.19.q_ref), channel_id=1, source_target_pairs={{0,8},{8,0},{16,24},{24,16},{32,40},{40,32},{48,56},{56,48},{64,72... | collective-permute-start | bytes 393224 | tf_op jit(solution)/shard_map/ppermute | solution.py:233
  102.6 0.7 copy-start.1
  111.7 7.2 %collective-permute-start.1 = (bf16[640,128]{1,0:T(8,128)(2,1)S(1)}, bf16[640,128]{1,0:T(8,128)(2,1)S(1)}, u32[]{:S(2)}, u32[]{:S(2)}) collective-permute-start(bf16[640,128]{1,0:T(8,128)(2,1)S(1)} %attend_partner.1), channel_id=1, source_target_pairs={{0,8},{8,0},{16,24},{24,16},{32,40},{40,32},{48,56},{56,48},{64,72... | collective-permute-start | bytes 491528 | tf_op jit(solution)/shard_map/ppermute | solution.py:233

commit v4 on v3

--- a/solution.py
+++ b/solution.py
@@ -36,7 +36,7 @@
     return lax.broadcasted_iota(i32, shape, dim)
 
 
-def pack_kernel(counts_ref, q_ref, k_ref, v_ref, out_ref, kv_ref):
+def pack_kernel(counts_ref, q_ref, k_ref, v_ref, out_ref, kv_ref, near_ref):
     me = lax.axis_index("ctx")
     row = counts_ref[pl.ds(me, 1), :].astype(f32)
     n = NCX * PARTS
@@ -55,6 +55,7 @@
     out_ref[...] = jnp.concatenate(pieces, axis=1).reshape(NCX, PARTS, SPAN)
     kv_ref[:, :HD] = k_ref[:MAIN, :]
     kv_ref[:, HD:] = v_ref[:MAIN, :]
+    near_ref[...] = counts_ref[...]
 
 
 def place_kernel(docs_ref, counts_ref, kv_ref, rest_ref, bias_ref, all_ref):
@@ -205,19 +206,16 @@
 def join_kernel(a_ref, b_ref, out_ref):
     sa = a_ref[GROUP * TOK :, :]
     sb = b_ref[GROUP * TOK :, :].astype(f32)
-
-    def stat(k):
-        return sum(sb[:, term * 2 * GROUP + k : term * 2 * GROUP + k + 1] for term in range(3))
-
+    sb = sb + pltpu.roll(sb, HD - 2 * GROUP, axis=1) + pltpu.roll(sb, HD - 4 * GROUP, axis=1)
+    top = jnp.maximum(sa, sb)
+    wa, wb = jnp.exp2((sa - top) * C2), jnp.exp2((sb - top) * C2)
+    wb = wb * pltpu.roll(sb, HD - GROUP, axis=1)
+    total = wa * pltpu.roll(sa, HD - GROUP, axis=1) + wb
+    wa, wb = wa / total, wb / total
     for h in range(GROUP):
-        top_a, top_b = sa[:, h : h + 1], stat(h)
-        top = jnp.maximum(top_a, top_b)
-        wa = jnp.exp2((top_a - top) * C2)
-        wb = jnp.exp2((top_b - top) * C2) * stat(GROUP + h)
-        total = sa[:, GROUP + h : GROUP + h + 1] * wa + wb
-        wa, wb = wa / total, wb / total
         rows = slice(h * TOK, (h + 1) * TOK)
-        out_ref[:, h * HD : (h + 1) * HD] = (a_ref[rows, :] * wa + b_ref[rows, :].astype(f32) * wb).astype(bf16)
+        half_a, half_b = a_ref[rows, :], b_ref[rows, :].astype(f32)
+        out_ref[:, h * HD : (h + 1) * HD] = (half_a * wa[:, h : h + 1] + half_b * wb[:, h : h + 1]).astype(bf16)
 
 
 VMEM = pl.BlockSpec(memory_space=pltpu.VMEM)
@@ -255,14 +253,15 @@
 
 def body(queries, keys, values, counts, doc_lengths):
     wide = GROUP * HD
-    packed, key_value = pl.pallas_call(
+    packed, key_value, sizes = pl.pallas_call(
         pack_kernel,
         out_shape=(
             pltpu.VMEM((NCX, PARTS, SPAN), bf16),
             pltpu.VMEM((MAIN, 2 * HD), bf16),
+            pltpu.VMEM((NCX, NCX), i32),
         ),
         in_specs=[VMEM, VMEM, VMEM, VMEM],
-        out_specs=(VMEM, VMEM),
+        out_specs=(VMEM, VMEM, VMEM),
         name="pack",
     )(counts, queries, keys, values)
     got = lax.all_to_all(
@@ -270,6 +269,7 @@
     )
     key_value = lax.all_gather(key_value, "ctx", axis=0, axis_index_groups=SIDES)
     got, key_value = lax.optimization_barrier((got, key_value))
+    sizes = near(sizes)
     query, rest = pl.pallas_call(
         unpack_kernel,
         out_shape=(
@@ -280,7 +280,7 @@
         out_specs=(VMEM, VMEM),
         compiler_params=LIMIT,
         name="unpack",
-    )(counts, near(got))
+    )(sizes, near(got))
     bias, key_value = pl.pallas_call(
         place_kernel,
         out_shape=(
@@ -291,7 +291,7 @@
         out_specs=(VMEM, VMEM),
         compiler_params=LIMIT,
         name="place",
-    )(doc_lengths, counts, near(key_value), near(rest))
+    )(doc_lengths, sizes, near(key_value), near(rest))
     bias, query, key_value = near(bias), near(query), near(key_value)
     partner = attend(1, bias, near(swap(query)), key_value)
     other = swap(partner)

time: 120 us -> 120 us (level)
  the two profiles are of different devices: /device:TPU:138 before, /device:TPU:136 now
where the time goes in v4:
time: 120 us; the launch traced here: 119 us
  blocking collectives  70.3 us (59%)
  starting transfers between devices  31.1 us (26%)
  Pallas kernels  10.7 us (9%)
  waiting for transfers between devices  6.56 us (5%)
    all_gather x1, blocking collectives, body(): lax.all_gather(key_value, 'ctx', axis=0, axis_index_groups=SIDES)  70.3 us
    all_to_all x1, starting transfers between devices, body(): got = lax.all_to_all(packed, 'ctx', split_axis=0, concat_axis=0, tiled=True)  27.2 us
    ppermute x2, waiting for transfers between devices, swap(): return lax.ppermute(x, 'ctx', [(i, i ^ 1) for i in range(NCX)])  6.56 us
    pallas_call x2, Pallas kernels, attend(): pl.pallas_call(functools.partial(attend_kernel, flip), out_shape=pltpu.VM...  5.93 us
    ppermute x2, starting transfers between devices, swap(): return lax.ppermute(x, 'ctx', [(i, i ^ 1) for i in range(NCX)])  3.84 us
  transfers between devices with their start and end apart: 3, of which 2 were waited for; matrix products, arithmetic and copies ran while one was open for 0% of the time, Pallas kernels for 4%

profile of v4, /device:TPU:136, one launch (start us, length us, event | category | flops | bytes accessed | tf_op | source)
XLA Modules:
  0.0 119.4 jit_solution(16259975040491660961)
XLA Ops:
  0.0 1.9 %pack.1 = (bf16[32,2,2176]{2,1,0:T(2,128)(2,1)}, bf16[127,256]{1,0:T(8,128)(2,1)S(1)}, s32[32,32]{1,0:T(8,128)S(1)}) custom-call(s32[32,32]{1,0:T(8,128)} %counts_ref.1, bf16[128,512]{1,0:T(8,128)(2,1)} %q_ref.1, bf16[128,128]{1,0:T(8,128)(2,1)} %k_ref.1, bf16[128,128]{1,0:T(8,128)(2,1)} %v_ref.1), custom_call_target="tpu_custom_call" | custom-call | tf_op jit(solution)/shard_map/pack/pallas_call | solution.py:256
  1.9 27.2 %all-to-all-start = ((bf16[32,2,2176]{2,1,0:T(2,128)(2,1)}), bf16[32,2,2176]{2,1,0:T(2,128)(2,1)S(1)}, u32[]{:S(2)}, u32[]{:S(2)}) async-start(bf16[32,2,2176]{2,1,0:T(2,128)(2,1)} %get-tuple-element.15), calls=%async_computation | async-start | bytes 557056 | tf_op jit(solution)/shard_map/all_to_all | solution.py:267
  29.2 70.3 %all-gather.1.kv_ref = bf16[16,127,256]{2,1,0:T(8,128)(2,1)S(1)} all-gather(bf16[1,127,256]{2,1,0:T(8,128)(2,1)S(1)} %bitcast.1), channel_id=2, replica_groups={{0,16,32,48,64,80,96,112,128,144,160,176,192,208,224,240},{8,24,40,56,7..., dimensions={0}, use_global_device_ids=true | all-gather | bytes 1105408 | tf_op jit(solution)/shard_map/all_gather | solution.py:270
  99.5 0.0 all-to-all-done.got_ref
  99.5 0.4 unpack.1
  99.9 1.9 %collective-permute-start = (bf16[512,128]{1,0:T(8,128)(2,1)S(1)}, bf16[512,128]{1,0:T(8,128)(2,1)S(1)}, u32[]{:S(2)}, u32[]{:S(2)}) collective-permute-start(bf16[512,128]{1,0:T(8,128)(2,1)S(1)} %get-tuple-element.21.q_ref), channel_id=1, source_target_pairs={{0,8},{8,0},{16,24},{24,16},{32,40},{40,32},{48,56},{56,48},{64,72... | collective-permute-start | bytes 393224 | tf_op jit(solution)/shard_map/ppermute | solution.py:231
  101.8 0.0 copy-start
  101.9 0.6 copy-done
  102.5 1.5 %place.1 = (f32[2,9,128,256]{3,2,1,0:T(8,128)S(1)}, bf16[2176,256]{1,0:T(8,128)(2,1)S(1)}) custom-call(s32[16]{0:T(128)S(1)} %copy-done, s32[32,32]{1,0:T(8,128)S(1)} %get-tuple-element.14.counts_ref, bf16[16,127,256]{2,1,0:T(8,128)(2,1)S(1)} %all-gather.1.kv_ref, bf16[16,256]{1,0:T(8,128)(2,1)S(1)} %get-tuple-element.19.rest_ref), custom_call_target="tpu_custom_call" | custom-call | tf_op jit(solution)/shard_map/place/pallas_call | solution.py:284
  104.0 4.2 %collective-permute-done.q_ref = bf16[512,128]{1,0:T(8,128)(2,1)S(1)} collective-permute-done((bf16[512,128]{1,0:T(8,128)(2,1)S(1)}, bf16[512,128]{1,0:T(8,128)(2,1)S(1)}, u32[]{:S(2)}, u32[]{:S(2)}) %collective-permute-start) | collective-permute-done | bytes 131104 | tf_op jit(solution)/shard_map/ppermute | solution.py:231
  108.2 3.0 %attend_partner.1 = bf16[640,128]{1,0:T(8,128)(2,1)S(1)} custom-call(f32[2,9,128,256]{3,2,1,0:T(8,128)S(1)} %get-tuple-element.20.bias_ref, bf16[512,128]{1,0:T(8,128)(2,1)S(1)} %collective-permute-done.q_ref, bf16[2176,256]{1,0:T(8,128)(2,1)S(1)} %get-tuple-element.22.kv_ref), custom_call_target="tpu_custom_call" | custom-call | flops 536870912 | bytes 1048576 | tf_op jit(solution)/shard_map/attend_partner/pallas_call | solution.py:235
  111.2 1.9 %collective-permute-start.1 = (bf16[640,128]{1,0:T(8,128)(2,1)S(1)}, bf16[640,128]{1,0:T(8,128)(2,1)S(1)}, u32[]{:S(2)}, u32[]{:S(2)}) collective-permute-start(bf16[640,128]{1,0:T(8,128)(2,1)S(1)} %attend_partner.1), channel_id=1, source_target_pairs={{0,8},{8,0},{16,24},{24,16},{32,40},{40,32},{48,56},{56,48},{64,72... | collective-permute-start | bytes 491528 | tf_op jit(solution)/shard_map/ppermute | solution.py:231
  113.1 2.9 %attend_own.1.a_ref = f32[640,128]{1,0:T(8,128)S(1)} custom-call(f32[2,9,128,256]{3,2,1,0:T(8,128)S(1)} %get-tuple-element.20.bias_ref, bf16[512,128]{1,0:T(8,128)(2,1)S(1)} %get-tuple-element.21.q_ref, bf16[2176,256]{1,0:T(8,128)(2,1)S(1)} %get-tuple-element.22.kv_ref), custom_call_target="tpu_custom_call" | custom-call | flops 536870912 | bytes 1048576 | tf_op jit(solution)/shard_map/attend_own/pallas_call | solution.py:235
  116.1 2.3 %collective-permute-done.1.b_ref = bf16[640,128]{1,0:T(8,128)(2,1)S(1)} collective-permute-done((bf16[640,128]{1,0:T(8,128)(2,1)S(1)}, bf16[640,128]{1,0:T(8,128)(2,1)S(1)}, u32[]{:S(2)}, u32[]{:S(2)}) %collective-permute-start.1) | collective-permute-done | bytes 163872 | tf_op jit(solution)/shard_map/ppermute | solution.py:231
  118.4 1.0 join.1
Async XLA Ops:
  1.9 97.6 %all-to-all-start = ((bf16[32,2,2176]{2,1,0:T(2,128)(2,1)}), bf16[32,2,2176]{2,1,0:T(2,128)(2,1)S(1)}, u32[]{:S(2)}, u32[]{:S(2)}) async-start(bf16[32,2,2176]{2,1,0:T(2,128)(2,1)} %get-tuple-element.15), calls=%async_computation | async-start | bytes 557056 | tf_op jit(solution)/shard_map/all_to_all | solution.py:267
  99.9 8.3 %collective-permute-start = (bf16[512,128]{1,0:T(8,128)(2,1)S(1)}, bf16[512,128]{1,0:T(8,128)(2,1)S(1)}, u32[]{:S(2)}, u32[]{:S(2)}) collective-permute-start(bf16[512,128]{1,0:T(8,128)(2,1)S(1)} %get-tuple-element.21.q_ref), channel_id=1, source_target_pairs={{0,8},{8,0},{16,24},{24,16},{32,40},{40,32},{48,56},{56,48},{64,72... | collective-permute-start | bytes 393224 | tf_op jit(solution)/shard_map/ppermute | solution.py:231
  101.8 0.7 copy-start
  111.2 7.2 %collective-permute-start.1 = (bf16[640,128]{1,0:T(8,128)(2,1)S(1)}, bf16[640,128]{1,0:T(8,128)(2,1)S(1)}, u32[]{:S(2)}, u32[]{:S(2)}) collective-permute-start(bf16[640,128]{1,0:T(8,128)(2,1)S(1)} %attend_partner.1), channel_id=1, source_target_pairs={{0,8},{8,0},{16,24},{24,16},{32,40},{40,32},{48,56},{56,48},{64,72... | collective-permute-start | bytes 491528 | tf_op jit(solution)/shard_map/ppermute | solution.py:231
